TPU v7x, 32 devices: a whole 2x2x4 slice. The times are simulated.
32 devices in a mesh: gx: 4 (over y, x), gy: 8 (over z, core).
Axes of the slice: x: 2, y: 2, z: 4, core: 2. Of those that a mesh axis runs over, the one named last changes fastest.
Arguments:
- thermal_field: bfloat16 [384, 384, 128], P('gx', 'gy'), may hold values from -6 to 6
- probe_range_east: bfloat16 [384, 128], P('gx'), may hold values from -0.3125 to 0.3125
- probe_range_north: bfloat16 [384, 128], P('gy'), may hold values from -0.3125 to 0.3125
- probe_range_upward: bfloat16 [128, 128], replicated, may hold values from -0.5 to 0.5
- gauss_kernel_east: bfloat16 [384, 384], replicated, may hold values from -0.3125 to 0.3125
- gauss_kernel_north: bfloat16 [384, 384], replicated, may hold values from -0.3125 to 0.3125
- gauss_kernel_upward: bfloat16 [384, 128], replicated, may hold values from -0.5 to 0.5
Outputs:
- factor_x: float32 [384, 128], P('gx')
- factor_y: float32 [384, 128], P('gy')
- factor_z: float32 [128, 128], replicated
- core_sketch: float32 [384, 384, 384], P('gx', None, 'gy')
All inputs are finite; a program needn't handle non-finite values.
Results may differ from a plain program's by a relative error of at most 0.0029.
Values may be sent and summed in bfloat16 or wider, within the bound.
A program may use at most 64 MiB of HBM per device.

v0:
```python
import jax
import jax.numpy as jnp
from jax import lax
from jax.sharding import PartitionSpec as P


def per_device(
    thermal_field,
    probe_range_east,
    probe_range_north,
    probe_range_upward,
    gauss_kernel_east,
    gauss_kernel_north,
    gauss_kernel_upward,
):
    highest = lax.Precision.HIGHEST
    line_tally, span_breadth, height_tally = thermal_field.shape
    width = probe_range_upward.shape[1]
    unrolled_tensor = thermal_field.reshape(line_tally * span_breadth, height_tally)
    weighted = jnp.dot(
        unrolled_tensor, probe_range_upward, preferred_element_type=jnp.float32
    ).reshape(line_tally, span_breadth, width)
    along_x = probe_range_east.astype(jnp.float32)
    along_y = probe_range_north.astype(jnp.float32)
    part_x = jnp.sum(weighted * along_y[None, :, :], axis=1)
    part_y = jnp.sum(weighted * along_x[:, None, :], axis=0)
    khatri = (
        (along_x[:, None, :] * along_y[None, :, :])
        .astype(jnp.bfloat16)
        .reshape(line_tally * span_breadth, width)
    )
    part_z = lax.dot_general(
        unrolled_tensor, khatri, (((0,), (0,)), ((), ())), preferred_element_type=jnp.float32
    )
    factor_x = lax.psum(part_x, "gy")
    factor_y = lax.psum(part_y, "gx")
    factor_z = lax.psum(part_z, ("gx", "gy"))
    mixer_zf = gauss_kernel_upward.astype(jnp.float32)
    mixer_yf = gauss_kernel_north.astype(jnp.float32)
    mixed = jnp.einsum(
        "ijl,ai->ajl",
        lax.all_to_all(thermal_field, "gx", split_axis=2, concat_axis=0, tiled=True),
        gauss_kernel_east,
        preferred_element_type=jnp.float32,
    )
    mixed = jnp.einsum(
        "ajl,cl->ajc",
        lax.all_to_all(mixed, "gx", split_axis=0, concat_axis=2, tiled=True),
        mixer_zf,
        precision=highest,
    )
    core_sketch = jnp.einsum(
        "ajc,bj->abc",
        lax.all_to_all(mixed, "gy", split_axis=2, concat_axis=1, tiled=True),
        mixer_yf,
        precision=highest,
    )
    return (factor_x, factor_y, factor_z, core_sketch)


def solution(mesh):
    in_specs = (P("gx", "gy", None), P("gx", None), P("gy", None), P(), P(), P(), P())
    out_specs = (P("gx", None), P("gy", None), P(), P("gx", None, "gy"))
    return jax.shard_map(
        per_device, mesh=mesh, in_specs=in_specs, out_specs=out_specs, check_vma=False
    )
```

profile of v0, /device:TPU:0, one launch (start us, length us, event | category | flops | bytes accessed | tf_op | source)
XLA Modules:
  0.0 390.0 jit_solution(121109077919172618)
XLA Ops:
  7.2 2.4 copy.38
  9.6 24.7 %all_to_all.54 = bf16[96,48,128]{0,1,2:T(8,128)(2,1)S(1)} all-to-all(bf16[96,48,128]{0,1,2:T(8,128)(2,1)S(1)} %copy.38), channel_id=1, replica_groups=mesh['gx'=4,'gy'=8] {'gx'}, dimensions={2} | all-to-all | bytes 2359296 | tf_op jit(solution)/shard_map/all_to_all | solution.py:42
  34.4 1.2 copy.40
  35.6 1.9 all_to_all.42
  37.5 2.1 fusion.5
  39.6 6.0 %copy.41 = f32[384,48,32]{1,2,0:T(8,128)} copy(f32[384,48,32]{0,1,2:T(8,128)S(1)} %fusion.5) | data formatting | bytes 4718592 | tf_op jit(solution)/shard_map/ijl,ai->ajl/dot_general | solution.py:40
  45.6 8.2 %reshape.20 = f32[4,1,147456]{2,1,0:T(1,128)} reshape(f32[384,32,48]{2,1,0:T(8,128)} %bitcast.42) | data formatting | bytes 4718592
  53.9 30.6 %all_to_all.55 = f32[4,1,147456]{2,1,0:T(1,128)S(1)} all-to-all(f32[4,1,147456]{2,1,0:T(1,128)} %reshape.20), channel_id=1, replica_groups=mesh['gx'=4,'gy'=8] {'gx'}, dimensions={0} | all-to-all | bytes 4718592 | tf_op jit(solution)/shard_map/all_to_all | solution.py:48
  84.4 0.5 broadcast.2
  84.9 8.3 %reduce = f32[4,147456]{1,0:T(4,128)} reduce(f32[4,1,147456]{2,1,0:T(1,128)S(1)} %all_to_all.55, f32[]{:T(128)} %broadcast.2), dimensions={1}, to_apply=%all_to_all.43.reduce_sub_computation | reduce | bytes 4718596 | tf_op jit(solution)/shard_map/all_to_all | solution.py:48
  93.2 7.3 %reshape.21 = f32[384,32,48]{2,1,0:T(8,128)} reshape(f32[4,147456]{1,0:T(4,128)} %reduce) | data formatting | bytes 4718592
  100.5 6.2 %copy.42 = f32[4,96,48,32]{1,3,0,2:T(8,128)S(1)} copy(f32[4,96,48,32]{2,3,1,0:T(8,128)} %bitcast.41) | data formatting | bytes 4718592 | tf_op jit(solution)/shard_map/all_to_all | solution.py:48
  106.7 7.1 %fusion.7 = f32[96,48,384]{2,0,1:T(8,128)} fusion(f32[96,48,128]{0,2,1:T(8,128)S(1)} %bitcast.43, bf16[384,128]{1,0:T(8,128)(2,1)S(1)} %copy-done.3), kind=kOutput, calls=%fused_computation.11 | convolution fusion | flops 2717908992 | bytes 9535488 | tf_op jit(solution)/shard_map/ajl,cl->ajc/dot_general | solution.py:46
  113.8 9.0 %copy.44 = f32[96,48,384]{0,1,2:T(8,128)} copy(f32[96,48,384]{2,0,1:T(8,128)} %fusion.7) | data formatting | bytes 14155776 | tf_op jit(solution)/shard_map/ajl,cl->ajc/dot_general | solution.py:46
  122.7 5.2 %all-to-all-start.2 = ((f32[96,48,384]{0,1,2:T(8,128)}), f32[96,48,384]{0,1,2:T(8,128)}, u32[]{:S(2)}, u32[]{:S(2)}) async-start(f32[96,48,384]{0,1,2:T(8,128)} %copy.44), calls=%async_computation.2 | async-start | bytes 18874368 | tf_op jit(solution)/shard_map/all_to_all | solution.py:54
  127.9 0.0 all-reduce.2.cloned.1.call-start
  128.0 1.1 fusion.3
  129.2 0.5 multiply_reduce_fusion
  129.8 15.4 %psum.22 = f32[48,128]{1,0:T(8,128)} all-reduce(f32[48,128]{1,0:T(8,128)S(1)} %get-tuple-element.20), channel_id=1, replica_groups=mesh['gx'=4,'gy'=8] {'gx'}, use_global_device_ids=true, to_apply=%region_3.0 | all-reduce | flops 6144 | bytes 49152 | tf_op jit(solution)/shard_map/psum | solution.py:36
  145.1 206.6 %psum.21 = f32[96,128]{1,0:T(8,128)} all-reduce(f32[96,128]{1,0:T(8,128)S(1)} %get-tuple-element.21), channel_id=1, replica_groups=mesh['gx'=4,'gy'=8] {'gy'}, use_global_device_ids=true, to_apply=%region_1.0 | all-reduce | flops 12288 | bytes 98304 | tf_op jit(solution)/shard_map/psum | solution.py:35
  351.7 1.6 copy.48
  353.3 10.1 %copy.46 = f32[96,8,48,48]{0,3,2,1:T(8,128)} copy(f32[96,8,48,48]{0,2,3,1:T(8,128)} %bitcast.13) | data formatting | bytes 14155776 | tf_op jit(solution)/shard_map/all_to_all | solution.py:54
  363.4 9.0 %copy.47 = f32[96,384,48]{1,2,0:T(8,128)} copy(f32[96,384,48]{0,2,1:T(8,128)} %bitcast.40) | data formatting | bytes 14155776 | tf_op jit(solution)/shard_map/all_to_all | solution.py:54
  372.4 10.7 %convolution_bitcast_fusion = f32[96,384,48]{1,2,0:T(8,128)} fusion(f32[96,384,48]{1,2,0:T(8,128)} %copy.47, bf16[384,384]{1,0:T(8,128)(2,1)S(1)} %copy-done), kind=kOutput, calls=%fused_computation | convolution fusion | flops 8153726976 | bytes 14450688 | tf_op jit(solution)/shard_map/ajc,bj->abc/dot_general | solution.py:52
  (19 shorter events, 0.1 us)
Async XLA Ops:
  7.2 365.3 %copy-start = (bf16[384,384]{1,0:T(8,128)(2,1)S(1)}, bf16[384,384]{1,0:T(8,128)(2,1)}, u32[]{:S(2)}) copy-start(bf16[384,384]{1,0:T(8,128)(2,1)} %param.12) | copy-start | bytes 884740
  34.4 3.1 copy-start.2
  100.5 6.2 %copy-start.3 = (bf16[384,128]{1,0:T(8,128)(2,1)S(1)}, bf16[384,128]{1,0:T(8,128)(2,1)}, u32[]{:S(2)}) copy-start(bf16[384,128]{1,0:T(8,128)(2,1)} %param.13) | copy-start | bytes 294916
  122.7 5.2 %copy-start.5 = (bf16[48,128]{1,0:T(8,128)(2,1)S(1)}, bf16[48,128]{1,0:T(8,128)(2,1)}, u32[]{:S(2)}) copy-start(bf16[48,128]{1,0:T(8,128)(2,1)} %param.9) | copy-start | bytes 36868
  122.7 5.3 %copy-start.4 = (bf16[96,128]{1,0:T(8,128)(2,1)S(1)}, bf16[96,128]{1,0:T(8,128)(2,1)}, u32[]{:S(2)}) copy-start(bf16[96,128]{1,0:T(8,128)(2,1)} %param.8) | copy-start | bytes 73732
  122.7 5.3 %copy-start.1 = (bf16[96,48,128]{2,1,0:T(8,128)(2,1)S(1)}, bf16[96,48,128]{2,1,0:T(8,128)(2,1)}, u32[]{:S(2)}) copy-start(bf16[96,48,128]{2,1,0:T(8,128)(2,1)} %param.7) | copy-start | bytes 3538948
  122.7 230.5 %all-to-all-start.2 = ((f32[96,48,384]{0,1,2:T(8,128)}), f32[96,48,384]{0,1,2:T(8,128)}, u32[]{:S(2)}, u32[]{:S(2)}) async-start(f32[96,48,384]{0,1,2:T(8,128)} %copy.44), calls=%async_computation.2 | async-start | bytes 18874368 | tf_op jit(solution)/shard_map/all_to_all | solution.py:54
  127.9 1.3 copy-start.6
  127.9 223.8 %all-reduce.2.cloned.1.call-start = ((), (), s32[]{:S(2)}) async-start(), calls=%async_computation.3 | async-start | bytes 131072 | tf_op jit(solution)/shard_map/psum | solution.py:37
Sparse Core Ops, SparseCore 0:
  134.9 161.8 all-reduce.1
where the time goes:
time: 391 us; the launch traced here: 390 us
  blocking collectives  277 us (71%)
  local copies, waits for them, and re-layouts  63.4 us (16%)
  matrix products  21.6 us (6%)
  between operations  14.1 us (4%)
  other arithmetic  8.29 us (2%)
  starting transfers between devices  5.21 us (1%)
    psum x1, blocking collectives, per_device(): factor_x = lax.psum(part_x, 'gy')  207 us
    all_to_all x1, blocking collectives, per_device(): lax.all_to_all(mixed, 'gx', split_axis=0, concat_axis=2, tiled=True)  30.6 us
    all_to_all x1, blocking collectives, per_device(): lax.all_to_all(thermal_field, 'gx', split_axis=2, concat_axis=0, tiled=True)  24.7 us
    unnamed x18, local copies, waits for them, and re-layouts  19.5 us
    all_to_all x2, local copies, waits for them, and re-layouts, per_device(): lax.all_to_all(mixed, 'gy', split_axis=2, concat_axis=1, tiled=True)  19.2 us
    psum x1, blocking collectives, per_device(): factor_y = lax.psum(part_y, 'gx')  15.4 us
    dot_general x1, matrix products, per_device(): jnp.einsum('ajc,bj->abc', lax.all_to_all(mixed, 'gy', split_axis=2, conca...  10.7 us
    dot_general x1, local copies, waits for them, and re-layouts, per_device(): jnp.einsum('ajl,cl->ajc', lax.all_to_all(mixed, 'gx', split_axis=0, conca...  8.98 us
  transfers between devices with their start and end apart: 2, of which 0 were waited for; matrix products, arithmetic and copies ran while one was open for 1% of the time, Pallas kernels for 0%

commit v1 on v0

--- a/solution.py
+++ b/solution.py
@@ -32,7 +32,9 @@
     part_z = lax.dot_general(
         unrolled_tensor, khatri, (((0,), (0,)), ((), ())), preferred_element_type=jnp.float32
     )
-    factor_x = lax.psum(part_x, "gy")
+    factor_x = part_x
+    for hop in (1, 2, 4):
+        factor_x = factor_x + lax.ppermute(factor_x, "gy", [(dev, dev ^ hop) for dev in range(8)])
     factor_y = lax.psum(part_y, "gx")
     factor_z = lax.psum(part_z, ("gx", "gy"))
     mixer_zf = gauss_kernel_upward.astype(jnp.float32)

time: 391 us -> 455 us (1.16)
  waiting for transfers between devices: 0.02 us -> 262 us
  blocking collectives: 277 us -> 70.7 us
  starting transfers between devices: 5.21 us -> 11.9 us
    psum x1 -> x0, blocking collectives: 207 us -> none  [per_device(): factor_x = lax.psum(part_x, 'gy')]
    ppermute x0 -> x3, waiting for transfers between devices: none -> 151 us  [per_device(): lax.ppermute(factor_x, 'gy', [(dev, dev ^ hop) for dev in range(8)])]
    psum x1, waiting for transfers between devices: 0.01 us -> 111 us  [per_device(): factor_z = lax.psum(part_z, ('gx', 'gy'))]
    ppermute x0 -> x3, starting transfers between devices: none -> 6.66 us  [per_device(): lax.ppermute(factor_x, 'gy', [(dev, dev ^ hop) for dev in range(8)])]
  transfers between devices with their start and end apart: 2 -> 5, of which waited for: 0 -> 3; matrix products, arithmetic and copies ran while one was open for 1% -> 1% of each run, Pallas kernels for 0% -> 0%
where the time goes in v1:
time: 455 us; the launch traced here: 453 us
  waiting for transfers between devices  262 us (58%)
  blocking collectives  70.7 us (16%)
  local copies, waits for them, and re-layouts  63.5 us (14%)
  matrix products  21.6 us (5%)
  between operations  14.2 us (3%)
  starting transfers between devices  11.9 us (3%)
  other arithmetic  8.94 us (2%)
    ppermute x3, waiting for transfers between devices, per_device(): lax.ppermute(factor_x, 'gy', [(dev, dev ^ hop) for dev in range(8)])  151 us
    psum x1, waiting for transfers between devices, per_device(): factor_z = lax.psum(part_z, ('gx', 'gy'))  111 us
    all_to_all x1, blocking collectives, per_device(): lax.all_to_all(mixed, 'gx', split_axis=0, concat_axis=2, tiled=True)  30.6 us
    all_to_all x1, blocking collectives, per_device(): lax.all_to_all(thermal_field, 'gx', split_axis=2, concat_axis=0, tiled=True)  24.7 us
    unnamed x18, local copies, waits for them, and re-layouts  19.5 us
    all_to_all x2, local copies, waits for them, and re-layouts, per_device(): lax.all_to_all(mixed, 'gy', split_axis=2, concat_axis=1, tiled=True)  19.2 us
    psum x1, blocking collectives, per_device(): factor_y = lax.psum(part_y, 'gx')  15.4 us
    dot_general x1, matrix products, per_device(): jnp.einsum('ajc,bj->abc', lax.all_to_all(mixed, 'gy', split_axis=2, conca...  10.7 us
  transfers between devices with their start and end apart: 5, of which 3 were waited for; matrix products, arithmetic and copies ran while one was open for 1% of the time, Pallas kernels for 0%

profile of v1, /device:TPU:0, one launch (start us, length us, event | category | flops | bytes accessed | tf_op | source)
XLA Modules:
  0.0 452.7 jit_solution(2490525639413589775)
XLA Ops:
  7.2 2.4 copy.38
  9.6 24.7 %all_to_all.54 = bf16[96,48,128]{0,1,2:T(8,128)(2,1)S(1)} all-to-all(bf16[96,48,128]{0,1,2:T(8,128)(2,1)S(1)} %copy.38), channel_id=1, replica_groups=mesh['gx'=4,'gy'=8] {'gx'}, dimensions={2} | all-to-all | bytes 2359296 | tf_op jit(solution)/shard_map/all_to_all | solution.py:44
  34.4 1.2 copy.40
  35.6 1.9 all_to_all.42
  37.5 2.1 fusion.5
  39.6 6.0 %copy.41 = f32[384,48,32]{1,2,0:T(8,128)} copy(f32[384,48,32]{0,1,2:T(8,128)S(1)} %fusion.5) | data formatting | bytes 4718592 | tf_op jit(solution)/shard_map/ijl,ai->ajl/dot_general | solution.py:42
  45.6 8.2 %reshape.20 = f32[4,1,147456]{2,1,0:T(1,128)} reshape(f32[384,32,48]{2,1,0:T(8,128)} %bitcast.42) | data formatting | bytes 4718592
  53.9 30.6 %all_to_all.55 = f32[4,1,147456]{2,1,0:T(1,128)S(1)} all-to-all(f32[4,1,147456]{2,1,0:T(1,128)} %reshape.20), channel_id=1, replica_groups=mesh['gx'=4,'gy'=8] {'gx'}, dimensions={0} | all-to-all | bytes 4718592 | tf_op jit(solution)/shard_map/all_to_all | solution.py:50
  85.0 8.3 %reduce = f32[4,147456]{1,0:T(4,128)} reduce(f32[4,1,147456]{2,1,0:T(1,128)S(1)} %all_to_all.55, f32[]{:T(128)} %broadcast.2), dimensions={1}, to_apply=%all_to_all.43.reduce_sub_computation | reduce | bytes 4718596 | tf_op jit(solution)/shard_map/all_to_all | solution.py:50
  93.2 7.3 %reshape.21 = f32[384,32,48]{2,1,0:T(8,128)} reshape(f32[4,147456]{1,0:T(4,128)} %reduce) | data formatting | bytes 4718592
  100.5 6.2 %copy.42 = f32[4,96,48,32]{1,3,0,2:T(8,128)S(1)} copy(f32[4,96,48,32]{2,3,1,0:T(8,128)} %bitcast.41) | data formatting | bytes 4718592 | tf_op jit(solution)/shard_map/all_to_all | solution.py:50
  106.7 7.1 %fusion.7 = f32[96,48,384]{2,0,1:T(8,128)} fusion(f32[96,48,128]{0,2,1:T(8,128)S(1)} %bitcast.43, bf16[384,128]{1,0:T(8,128)(2,1)S(1)} %copy-done.3), kind=kOutput, calls=%fused_computation.11 | convolution fusion | flops 2717908992 | bytes 9535488 | tf_op jit(solution)/shard_map/ajl,cl->ajc/dot_general | solution.py:48
  113.8 9.0 %copy.44 = f32[96,48,384]{0,1,2:T(8,128)} copy(f32[96,48,384]{2,0,1:T(8,128)} %fusion.7) | data formatting | bytes 14155776 | tf_op jit(solution)/shard_map/ajl,cl->ajc/dot_general | solution.py:48
  122.7 5.2 %all-to-all-start.2 = ((f32[96,48,384]{0,1,2:T(8,128)}), f32[96,48,384]{0,1,2:T(8,128)}, u32[]{:S(2)}, u32[]{:S(2)}) async-start(f32[96,48,384]{0,1,2:T(8,128)} %copy.44), calls=%async_computation.2 | async-start | bytes 18874368 | tf_op jit(solution)/shard_map/all_to_all | solution.py:56
  129.0 2.0 collective-permute-done
  131.0 1.7 collective-permute-start.1
  132.7 149.0 %collective-permute-done.1 = f32[96,128]{1,0:T(8,128)S(1)} collective-permute-done((f32[96,128]{1,0:T(8,128)S(1)}, f32[96,128]{1,0:T(8,128)S(1)}, u32[]{:S(2)}, u32[]{:S(2)}) %collective-permute-start.1) | collective-permute-done | bytes 49184 | tf_op jit(solution)/shard_map/ppermute | solution.py:37
  281.7 4.6 %collective-permute-start.2 = (f32[96,128]{1,0:T(8,128)S(1)}, f32[96,128]{1,0:T(8,128)S(1)}, u32[]{:S(2)}, u32[]{:S(2)}) collective-permute-start(f32[96,128]{1,0:T(8,128)S(1)} %add.14), channel_id=1, source_target_pairs={{0,4},{1,5},{2,6},{3,7},{4,0},{5,1},{6,2},{7,3},{8,12},{9,13},{10,... | collective-permute-start | bytes 147464 | tf_op jit(solution)/shard_map/ppermute | solution.py:37
  287.5 15.4 %psum.14 = f32[48,128]{1,0:T(8,128)} all-reduce(f32[48,128]{1,0:T(8,128)S(1)} %get-tuple-element.20), channel_id=1, replica_groups=mesh['gx'=4,'gy'=8] {'gx'}, use_global_device_ids=true, to_apply=%region_2.0 | all-reduce | flops 6144 | bytes 49152 | tf_op jit(solution)/shard_map/psum | solution.py:38
  302.8 110.9 %all-reduce.2.cloned.1.call-done = f32[128,128]{0,1:T(8,128)} async-done(((f32[128,128]{0,1:T(8,128)}), f32[128,128]{0,1:T(8,128)}) %all-reduce.2.cloned.1.call-update) | async-done | bytes 65552 | tf_op jit(solution)/shard_map/psum | solution.py:39
  413.7 1.6 copy.48
  415.9 10.1 %copy.46 = f32[96,8,48,48]{0,3,2,1:T(8,128)} copy(f32[96,8,48,48]{0,2,3,1:T(8,128)} %bitcast.13) | data formatting | bytes 14155776 | tf_op jit(solution)/shard_map/all_to_all | solution.py:56
  426.0 9.1 %copy.47 = f32[96,384,48]{1,2,0:T(8,128)} copy(f32[96,384,48]{0,2,1:T(8,128)} %bitcast.40) | data formatting | bytes 14155776 | tf_op jit(solution)/shard_map/all_to_all | solution.py:56
  435.1 10.7 %convolution_bitcast_fusion = f32[96,384,48]{1,2,0:T(8,128)} fusion(f32[96,384,48]{1,2,0:T(8,128)} %copy.47, bf16[384,384]{1,0:T(8,128)(2,1)S(1)} %copy-done), kind=kOutput, calls=%fused_computation | convolution fusion | flops 8153726976 | bytes 14450688 | tf_op jit(solution)/shard_map/ajc,bj->abc/dot_general | solution.py:54
  (27 shorter events, 3.3 us)
Async XLA Ops:
  7.2 427.9 %copy-start = (bf16[384,384]{1,0:T(8,128)(2,1)S(1)}, bf16[384,384]{1,0:T(8,128)(2,1)}, u32[]{:S(2)}) copy-start(bf16[384,384]{1,0:T(8,128)(2,1)} %param.12) | copy-start | bytes 884740
  34.4 3.1 copy-start.2
  100.5 6.2 %copy-start.3 = (bf16[384,128]{1,0:T(8,128)(2,1)S(1)}, bf16[384,128]{1,0:T(8,128)(2,1)}, u32[]{:S(2)}) copy-start(bf16[384,128]{1,0:T(8,128)(2,1)} %param.13) | copy-start | bytes 294916
  122.7 5.2 %copy-start.5 = (bf16[48,128]{1,0:T(8,128)(2,1)S(1)}, bf16[48,128]{1,0:T(8,128)(2,1)}, u32[]{:S(2)}) copy-start(bf16[48,128]{1,0:T(8,128)(2,1)} %param.9) | copy-start | bytes 36868
  122.7 5.3 %copy-start.4 = (bf16[96,128]{1,0:T(8,128)(2,1)S(1)}, bf16[96,128]{1,0:T(8,128)(2,1)}, u32[]{:S(2)}) copy-start(bf16[96,128]{1,0:T(8,128)(2,1)} %param.8) | copy-start | bytes 73732
  122.7 5.3 %copy-start.1 = (bf16[96,48,128]{2,1,0:T(8,128)(2,1)S(1)}, bf16[96,48,128]{2,1,0:T(8,128)(2,1)}, u32[]{:S(2)}) copy-start(bf16[96,48,128]{2,1,0:T(8,128)(2,1)} %param.7) | copy-start | bytes 3538948
  122.7 5.3 %copy-start.6 = (bf16[128,128]{1,0:T(8,128)(2,1)S(1)}, bf16[128,128]{1,0:T(8,128)(2,1)}, u32[]{:S(2)}) copy-start(bf16[128,128]{1,0:T(8,128)(2,1)} %param.10) | copy-start | bytes 98308
  122.7 293.2 %all-to-all-start.2 = ((f32[96,48,384]{0,1,2:T(8,128)}), f32[96,48,384]{0,1,2:T(8,128)}, u32[]{:S(2)}, u32[]{:S(2)}) async-start(f32[96,48,384]{0,1,2:T(8,128)} %copy.44), calls=%async_computation.2 | async-start | bytes 18874368 | tf_op jit(solution)/shard_map/all_to_all | solution.py:56
  127.9 285.8 %all-reduce.2.cloned.1.call-start = ((), (), s32[]{:S(2)}) async-start(), calls=%async_computation.3 | async-start | bytes 131072 | tf_op jit(solution)/shard_map/psum | solution.py:39
  128.6 2.4 collective-permute-start
  131.0 150.7 %collective-permute-start.1 = (f32[96,128]{1,0:T(8,128)S(1)}, f32[96,128]{1,0:T(8,128)S(1)}, u32[]{:S(2)}, u32[]{:S(2)}) collective-permute-start(f32[96,128]{1,0:T(8,128)S(1)} %add.13), channel_id=1, source_target_pairs={{0,2},{1,3},{2,0},{3,1},{4,6},{5,7},{6,4},{7,5},{8,10},{9,11},{10,... | collective-permute-start | bytes 147464 | tf_op jit(solution)/shard_map/ppermute | solution.py:37
  281.7 133.5 %collective-permute-start.2 = (f32[96,128]{1,0:T(8,128)S(1)}, f32[96,128]{1,0:T(8,128)S(1)}, u32[]{:S(2)}, u32[]{:S(2)}) collective-permute-start(f32[96,128]{1,0:T(8,128)S(1)} %add.14), channel_id=1, source_target_pairs={{0,4},{1,5},{2,6},{3,7},{4,0},{5,1},{6,2},{7,3},{8,12},{9,13},{10,... | collective-permute-start | bytes 147464 | tf_op jit(solution)/shard_map/ppermute | solution.py:37
Sparse Core Ops, SparseCore 0:
  287.6 126.0 all-reduce.1
